TPU v7x, 32 devices: a whole 2x2x4 slice. The times are simulated.
32 devices in a mesh: groups: 2 (over x), ep: 16 (over z, y, core).
Axes of the slice: x: 2, y: 2, z: 4, core: 2. Of those that a mesh axis runs over, the one named last changes fastest.
Arguments:
- inputs: float32 [64, 6144], P(('groups', 'ep')), parts along dimension 0, may hold values from -6 to 6
- norm_gain: float32 [6144], replicated, may hold values from 0.5 to 1.5
- dense_gate: bfloat16 [6144, 12288], P(None, 'ep'), may hold values from -0.078125 to 0.078125
- dense_up: bfloat16 [6144, 12288], P(None, 'ep'), may hold values from -0.078125 to 0.078125
- dense_down: bfloat16 [12288, 6144], P('ep'), may hold values from -0.0546875 to 0.0546875
- expert_gate: bfloat16 [6144, 32768], P(None, 'ep'), may hold values from -0.078125 to 0.078125
- expert_up: bfloat16 [6144, 32768], P(None, 'ep'), may hold values from -0.078125 to 0.078125
- expert_down: bfloat16 [32768, 6144], P('ep'), may hold values from -0.125 to 0.125
- expert_ids: int32 [64, 12], P('groups'), parts along dimension 0, may hold values from 0 to 16, all different within a row; in each aligned block of 2 rows (0 to 1, 2 to 3, ...) at most 2 rows name the same one
- route_weights: int32 [64, 12], P('groups'), parts along dimension 0, may hold values from 1 to 1024
- out_gain: float32 [6144], replicated, may hold values from 0.5 to 1.5
Outputs:
- result: float32 [64, 6144], P(('groups', 'ep')), parts along dimension 0
There are 2 independent parts, one for each index of `groups`. A program takes and returns all parts, laid end to end along the dimension named above; an argument that names none is the same for every part. Nothing has to cross between parts.
Inputs may be any that keep to these rules, and one draw needn't show every extreme that they name: `expert_ids`: each row names 12 different values; in the rows of one device (aligned blocks of 2 rows) no value is named by more than 2 rows, and in every draw some value is named by exactly 2 rows of one device.
All inputs are finite; a program needn't handle non-finite values.
Results may differ from a plain program's by a relative error of at most 0.0031.
Values may be sent and summed in bfloat16 or wider, within the bound.
A program may use at most 192 MiB of HBM per device.

v0:
```python
import jax
import jax.numpy as jnp
from jax import lax
from jax.sharding import PartitionSpec as P

EXPERTS = 16
MOST = 2


def rms_scale(values):
    return values * lax.rsqrt(jnp.mean(values * values, axis=-1, keepdims=True) + 1e-06)


def slot_table(expert_ids, weights_all, expert, blocks, block_rows):
    matches = expert_ids == expert
    picked = jnp.any(matches, axis=1).reshape(blocks, block_rows)
    weight = jnp.sum(jnp.where(matches, weights_all, 0.0), axis=1).reshape(blocks, block_rows)
    ranking = jnp.cumsum(picked.astype(jnp.int32), axis=1) - 1
    position = lax.broadcasted_iota(jnp.int32, (blocks, block_rows), 1)
    row_cols = []
    weight_cols = []
    for column in range(MOST):
        chosen = picked & (ranking == column)
        row_cols.append(jnp.sum(jnp.where(chosen, position, 0), axis=1))
        weight_cols.append(jnp.sum(jnp.where(chosen, weight, 0.0), axis=1))
    offsets = lax.broadcasted_iota(jnp.int32, (blocks, 1), 0) * block_rows
    slot_rows = (jnp.stack(row_cols, axis=1) + offsets).reshape(-1)
    slot_weight = jnp.stack(weight_cols, axis=1).reshape(-1)
    return (slot_rows, slot_weight)


def on_device(
    inputs,
    norm_gain,
    dense_gate,
    dense_up,
    dense_down,
    expert_gate,
    expert_up,
    expert_down,
    expert_ids,
    route_weights,
    out_gain,
):
    devices = lax.axis_size("ep")
    rows_own = inputs.shape[0]
    width = inputs.shape[1]
    slices = devices // EXPERTS
    my_index = lax.axis_index("ep")
    expert = my_index // slices
    hidden_in = (rms_scale(inputs) * norm_gain).astype(jnp.bfloat16)
    gathered = lax.all_gather(hidden_in, "ep", axis=0, tiled=True)
    gate = jnp.dot(gathered, dense_gate, preferred_element_type=jnp.float32)
    upper = jnp.dot(gathered, dense_up, preferred_element_type=jnp.float32)
    dense_hidden = (jax.nn.silu(gate) * upper).astype(jnp.bfloat16)
    weights_all = route_weights.astype(jnp.float32) / 1024.0
    slot_rows, slot_weight = slot_table(expert_ids, weights_all, expert, devices, rows_own)
    picked_in = gathered[slot_rows]
    e_gate = jnp.dot(picked_in, expert_gate, preferred_element_type=jnp.float32)
    e_upper = jnp.dot(picked_in, expert_up, preferred_element_type=jnp.float32)
    e_hidden = (jax.nn.silu(e_gate) * e_upper).astype(jnp.bfloat16)
    partial_value = (
        jnp.dot(e_hidden, expert_down, preferred_element_type=jnp.float32) * slot_weight[:, None]
    )
    own_start = my_index * rows_own
    own_ids = lax.dynamic_slice_in_dim(expert_ids, own_start, rows_own, 0)
    own_weights = lax.dynamic_slice_in_dim(weights_all, own_start, rows_own, 0)
    zero_weight = jnp.sum(jnp.where(own_ids == EXPERTS, own_weights, 0.0), axis=1)
    local_moe = zero_weight[:, None] * hidden_in.astype(jnp.float32)
    spread = jnp.zeros((gathered.shape[0], width), jnp.float32).at[slot_rows].add(partial_value)
    summed = lax.psum_scatter(
        jnp.dot(dense_hidden, dense_down, preferred_element_type=jnp.float32) + spread,
        "ep",
        scatter_dimension=0,
        tiled=True,
    )
    joined = summed + local_moe
    return inputs + rms_scale(joined) * out_gain


def solution(mesh):
    placed = (
        P(("groups", "ep"), None),
        P(),
        P(None, "ep"),
        P(None, "ep"),
        P("ep", None),
        P(None, "ep"),
        P(None, "ep"),
        P("ep", None),
        P("groups", None),
        P("groups", None),
        P(),
    )
    return jax.shard_map(
        on_device, mesh=mesh, in_specs=placed, out_specs=P(("groups", "ep"), None), check_vma=False
    )
```

profile of v0, /device:TPU:0, one launch (start us, length us, event | category | flops | bytes accessed | tf_op | source)
XLA Modules:
  0.0 182.8 jit_solution(16079961452170177742)
XLA Ops:
  6.5 0.0 all-reduce.3.cloned.1.call-start
  6.5 1.0 multiply_reduce_fusion.1
  7.5 0.9 fusion.30
  8.4 24.2 %all-gather = bf16[16,2,6144]{2,1,0:T(2,128)(2,1)S(1)} all-gather(bf16[1,2,6144]{2,1,0:T(2,128)(2,1)S(1)} %fusion.30), channel_id=1, replica_groups=mesh['groups'=2,'ep'=16] {'ep'}, dimensions={0}, use_global_device_ids=true | all-gather | bytes 417792 | tf_op jit(solution)/shard_map/all_gather | solution.py:52
  32.6 0.1 reshape.80
  32.8 0.7 select_reduce_fusion.3
  33.5 0.1 reshape.62
  33.6 0.1 reshape.61
  33.7 0.2 reduce_window_sum.11
  33.9 0.1 select_reduce_fusion.2
  34.0 0.1 select_reduce_fusion.4
  34.2 0.1 copy.16
  34.2 0.1 add.76
  34.4 5.3 %fusion.18 = f32[32,768]{1,0:T(8,128)S(1)} fusion(bf16[32,6144]{1,0:T(8,128)(2,1)S(1)} %reshape.80, bf16[6144,768]{1,0:T(8,128)(2,1)} %param.13), kind=kOutput, calls=%fused_computation.46 | convolution fusion | flops 301989888 | bytes 9928704 | tf_op jit(solution)/shard_map/dot_general | solution.py:53
  39.7 0.8 gather_fusion
  40.5 0.1 copy.17
  40.6 0.1 mul.91
  40.7 10.4 %fusion.19 = f32[32,2048]{1,0:T(8,128)S(1)} fusion(bf16[32,6144]{1,0:T(8,128)(2,1)S(1)} %gather_fusion, bf16[6144,2048]{1,0:T(8,128)(2,1)} %param.16), kind=kOutput, calls=%fused_computation.47 | convolution fusion | flops 805306368 | bytes 25821184 | tf_op jit(solution)/shard_map/dot_general | solution.py:59
  51.1 10.2 %fusion.2 = f32[32,6144]{1,0:T(8,128)S(1)} fusion(bf16[768,6144]{1,0:T(8,128)(2,1)} %param.15, bf16[32,6144]{1,0:T(8,128)(2,1)S(1)} %reshape.80, bf16[6144,768]{1,0:T(8,128)(2,1)} %param.14, f32[32,768]{1,0:T(8,128)S(1)} %fusion.18), kind=kOutput, calls=%fused_computation.7 | convolution fusion | flops 604127232 | bytes 20152320 | tf_op jit(solution)/shard_map/dot_general | solution.py:72
  61.3 0.0 copy-start.5
  61.3 0.0 copy-start.3
  61.3 0.0 copy-start.1
  61.3 0.0 copy-start.2
  61.3 0.0 copy-start.4
  61.3 19.9 %convolution_multiply_fusion = f32[32,6144]{1,0:T(8,128)S(1)} fusion(bf16[2048,6144]{1,0:T(8,128)(2,1)} %param.18, bf16[32,6144]{1,0:T(8,128)(2,1)S(1)} %gather_fusion, bf16[6144,2048]{1,0:T(8,128)(2,1)} %param.17, f32[32]{0:T(128)S(1)} %mul.91, f32[32,2048]{1,0:T(8,128)S(1)} %fusion.19), kind=kOutput, calls=%fused_computation.2 | convolution fusion | flops 1611202560 | bytes 51773568 | tf_op jit(solution)/shard_map/dot_general | solution.py:63
  81.2 1.8 scatter_fusion
  83.1 0.0 copy-start
  83.1 0.9 copy-done
  84.0 0.0 all-reduce.3.cloned.1.call-update
  84.0 0.0 copy-done.5
  84.0 0.6 dynamic-slice
  85.2 0.0 copy-done.3
  85.2 0.1 select_reduce_fusion
  85.3 88.7 %all-reduce.3.cloned.1.call-done = f32[32,6144]{1,0:T(8,128)} async-done(((f32[32,6144]{1,0:T(8,128)}), f32[32,6144]{1,0:T(8,128)}) %all-reduce.3.cloned.1.call-update) | async-done | bytes 786448
  174.0 0.0 copy-done.1
  174.0 0.0 copy-done.2
  174.0 1.2 multiply_reduce_fusion
  175.2 0.0 copy-done.4
  175.2 0.7 multiply_add_fusion
  (9 shorter events, 0.1 us)
Async XLA Ops:
  6.5 167.5 %all-reduce.3.cloned.1.call-start = ((), (), s32[]{:S(2)}) async-start(), calls=%async_computation | async-start | bytes 1572864
  61.3 22.7 %copy-start.5 = (u32[32]{0:T(128)S(1)}, u32[32]{0:T(128)}, u32[]{:S(2)}) copy-start(u32[32]{0:T(128)} %constant.56) | copy-start | bytes 388
  61.3 24.0 %copy-start.3 = (s32[32,12]{0,1:T(8,128)S(1)}, s32[32,12]{0,1:T(8,128)}, u32[]{:S(2)}) copy-start(s32[32,12]{0,1:T(8,128)} %param.19) | copy-start | bytes 4612
  61.3 112.7 %copy-start.1 = (f32[2,6144]{1,0:T(2,128)S(1)}, f32[2,6144]{1,0:T(2,128)}, u32[]{:S(2)}) copy-start(f32[2,6144]{1,0:T(2,128)} %param.11) | copy-start | bytes 147460
  61.3 112.7 %copy-start.2 = (f32[6144]{0:T(1024)S(1)}, f32[6144]{0:T(1024)}, u32[]{:S(2)}) copy-start(f32[6144]{0:T(1024)} %param.12) | copy-start | bytes 73732
  61.3 113.9 %copy-start.4 = (f32[6144]{0:T(1024)S(1)}, f32[6144]{0:T(1024)}, u32[]{:S(2)}) copy-start(f32[6144]{0:T(1024)} %param.21) | copy-start | bytes 73732
  83.1 0.9 copy-start
Sparse Core Ops, SparseCore 0:
  84.1 89.8 all-reduce.2
where the time goes:
time: 183 us
  waiting for transfers between devices  88.7 us (48%)
  matrix products  45.8 us (25%)
  blocking collectives  24.2 us (13%)
  between operations  14.2 us (8%)
  other arithmetic  6.89 us (4%)
  local copies, waits for them, and re-layouts  2.98 us (2%)
    unnamed x2, waiting for transfers between devices  88.7 us
    all_gather x1, blocking collectives, on_device(): gathered = lax.all_gather(hidden_in, 'ep', axis=0, tiled=True)  24.2 us
    dot_general x1, matrix products, on_device(): jnp.dot(e_hidden, expert_down, preferred_element_type=jnp.float32)  19.9 us
    dot_general x1, matrix products, on_device(): e_gate = jnp.dot(picked_in, expert_gate, preferred_element_type=jnp.float32)  10.4 us
    dot_general x1, matrix products, on_device(): jnp.dot(dense_hidden, dense_down, preferred_element_type=jnp.float32)  10.2 us
    dot_general x1, matrix products, on_device(): gate = jnp.dot(gathered, dense_gate, preferred_element_type=jnp.float32)  5.33 us
  transfers between devices with their start and end apart: 1, of which 1 were waited for; matrix products, arithmetic and copies ran while one was open for 0% of the time, Pallas kernels for 0%

commit v1 on v0

v1 whole, which is shorter than its diff:
```python
import functools

import jax
import jax.numpy as jnp
from jax import lax
from jax.experimental import pallas as pl
from jax.experimental.pallas import tpu as pltpu
from jax.sharding import PartitionSpec as P

EXPERTS = 16
WIDE = 256
QUARTERS = 4
VMEM_TOTAL = 66_900_000


def kernel(
    cfg,
    inputs_hbm,
    norm_gain_hbm,
    dense_gate,
    dense_up,
    dense_down,
    expert_gate,
    expert_up,
    expert_down,
    ids_hbm,
    route_hbm,
    out_gain_hbm,
    out_ref,
    inputs,
    norm_gain,
    out_gain,
    ids,
    route,
    ring,
    spare,
    landed,
    rows_in,
    dense_hidden,
    expert_hidden,
    by_device,
    scale,
    outgoing,
    incoming,
    small_sem,
    ring_sem,
    spare_sem,
    gather_send,
    gather_recv,
    reduce_send,
    reduce_recv,
):
    n, own, slots, n_dense, n_expert, n_down = cfg
    rows = n * own
    width = inputs.shape[1]
    k_dense = dense_down.shape[0]
    k_expert = expert_down.shape[0]
    k_both = k_dense + k_expert
    n_up = n_dense + n_expert
    total = n_up + n_down
    me = lax.axis_index("ep")
    expert = me // (n // EXPERTS)

    def up_copies(unit, first, gate, upper):
        slot = lax.rem(unit, slots)
        columns = pl.ds(pl.multiple_of((unit - first) * WIDE, WIDE), WIDE)
        return [
            pltpu.make_async_copy(
                source.at[:, columns], ring.at[slot, which], ring_sem.at[slot, which]
            )
            for which, source in enumerate((gate, upper))
        ]

    def down_copies(unit, quarter):
        slot = lax.rem(unit, slots)
        start = ((unit - n_up) * QUARTERS + quarter) * WIDE
        columns = pl.ds(pl.multiple_of(start, WIDE), WIDE)
        base = (quarter % 2) * k_both
        return [
            pltpu.make_async_copy(
                dense_down.at[:, columns],
                ring.at[slot, quarter // 2, pl.ds(base, k_dense)],
                ring_sem.at[slot, 2 * quarter],
            ),
            pltpu.make_async_copy(
                expert_down.at[:, columns],
                ring.at[slot, quarter // 2, pl.ds(base + k_dense, k_expert)],
                ring_sem.at[slot, 2 * quarter + 1],
            ),
        ]

    def start_unit(unit):
        @pl.when(unit < n_dense)
        def _():
            for copy in up_copies(unit, 0, dense_gate, dense_up):
                copy.start()

        @pl.when((unit >= n_dense) & (unit < n_up))
        def _():
            for copy in up_copies(unit, n_dense, expert_gate, expert_up):
                copy.start()

        @pl.when((unit >= n_up) & (unit < total))
        def _():
            for quarter in range(QUARTERS):
                for copy in down_copies(unit, quarter):
                    copy.start()

    small = [
        pltpu.make_async_copy(source, target, small_sem.at[at])
        for at, (source, target) in enumerate(
            (
                (inputs_hbm, inputs),
                (norm_gain_hbm, norm_gain),
                (ids_hbm, ids),
                (route_hbm, route),
                (out_gain_hbm, out_gain),
            )
        )
    ]
    for copy in small:
        copy.start()
    if n_dense == 0:
        spare_copies = [
            pltpu.make_async_copy(source, spare.at[at], spare_sem.at[at])
            for at, source in enumerate((dense_gate, dense_up))
        ]
        for copy in spare_copies:
            copy.start()
    lax.fori_loop(0, min(slots, total), lambda unit, _: start_unit(unit), None)

    barrier = pltpu.get_barrier_semaphore()

    def greet(offset, _):
        pl.semaphore_signal(barrier, inc=1, device_id={"ep": lax.rem(me + offset, n)})

    lax.fori_loop(1, n, greet, None)

    for copy in small:
        copy.wait()
    value = inputs[...]
    square = jnp.mean(value * value, axis=-1, keepdims=True)
    hidden_own = (value * lax.rsqrt(square + 1e-06) * norm_gain[...]).astype(jnp.bfloat16)
    landed[0] = hidden_own
    pl.semaphore_wait(barrier, n - 1)

    def gather_copy(offset):
        return pltpu.make_async_remote_copy(
            src_ref=landed.at[0],
            dst_ref=landed.at[n - offset],
            send_sem=gather_send.at[offset],
            recv_sem=gather_recv.at[n - offset],
            device_id={"ep": lax.rem(me + offset, n)},
        )

    lax.fori_loop(1, n, lambda offset, _: gather_copy(offset).start(), None)

    weights_all = route[...].astype(jnp.float32) / 1024.0
    named = jnp.sum(jnp.where(ids[...] == expert, weights_all, 0.0), axis=1, keepdims=True)
    zeros = jnp.sum(jnp.where(ids[...] == EXPERTS, weights_all, 0.0), axis=1, keepdims=True)
    named = jnp.broadcast_to(named, (rows, WIDE))
    zeros = jnp.broadcast_to(zeros, (rows, WIDE))
    for block in range(n):
        lines = slice(block * own, (block + 1) * own)
        by_device[0, block] = named[lines]
        by_device[1, block] = zeros[lines]
    for block in range(n):
        scale[block * own : (block + 1) * own] = by_device[0, lax.rem(me + block, n)]
    zero_weight = by_device[1, me][:, :1]

    def landing(offset, _):
        gather_copy(n - offset).wait_recv()

    lax.fori_loop(1, n, landing, None)
    for block in range(n):
        rows_in[block * own : (block + 1) * own] = landed[block]

    def gated(gate, upper):
        return (gate / (1.0 + jnp.exp(-gate)) * upper).astype(jnp.bfloat16)

    def product(left, right):
        return jnp.dot(left, right, preferred_element_type=jnp.float32)

    def up_unit(first, gate_hbm, upper_hbm, hidden):
        def body(unit, _):
            slot = lax.rem(unit, slots)
            copies = up_copies(unit, first, gate_hbm, upper_hbm)
            copies[0].wait()
            gate = product(rows_in[...], ring[slot, 0])
            copies[1].wait()
            upper = product(rows_in[...], ring[slot, 1])
            columns = pl.ds(pl.multiple_of((unit - first) * WIDE, WIDE), WIDE)
            hidden[:, columns] = gated(gate, upper)
            start_unit(unit + slots)

        return body

    if n_dense == 0:
        for copy in spare_copies:
            copy.wait()
        dense_hidden[...] = gated(
            product(rows_in[...], spare[0]), product(rows_in[...], spare[1])
        )
    else:
        lax.fori_loop(0, n_dense, up_unit(0, dense_gate, dense_up, dense_hidden), None)
    lax.fori_loop(n_dense, n_up, up_unit(n_dense, expert_gate, expert_up, expert_hidden), None)

    def reduce_copy(offset, part):
        source, target = outgoing.at[offset], incoming.at[n - offset]
        if part is not None:
            source, target = outgoing.at[offset, part], incoming.at[n - offset, part]
        return pltpu.make_async_remote_copy(
            src_ref=source,
            dst_ref=target,
            send_sem=reduce_send.at[offset],
            recv_sem=reduce_recv.at[n - offset],
            device_id={"ep": lax.rem(me + offset, n)},
        )

    def down_unit(unit, _):
        slot = lax.rem(unit, slots)
        weight = scale[...]
        for quarter in range(QUARTERS):
            for copy in down_copies(unit, quarter):
                copy.wait()
            base = (quarter % 2) * k_both
            block = ring.at[slot, quarter // 2]
            part_sum = product(dense_hidden[...], block[base : base + k_dense])
            part_sum += weight * product(
                expert_hidden[...], block[base + k_dense : base + k_both]
            )
            part = (unit - n_up) * (QUARTERS // 2) + quarter // 2
            side = (quarter % 2) * WIDE
            for to in range(n):
                outgoing[to, part, :, side : side + WIDE] = part_sum[
                    to * own : (to + 1) * own
                ].astype(jnp.bfloat16)
            if quarter % 2 == 1:
                lax.fori_loop(
                    1, n, lambda offset, _: reduce_copy(offset, part).start(), None
                )
        start_unit(unit + slots)

    lax.fori_loop(n_up, total, down_unit, None)

    def arrived(offset, _):
        reduce_copy(n - offset, None).wait_recv()

    lax.fori_loop(1, n, arrived, None)
    parts = []
    chunk = 2 * WIDE
    squares = jnp.zeros((own, 1), jnp.float32)
    for part in range(width // chunk):
        columns = slice(part * chunk, (part + 1) * chunk)
        piece = zero_weight * landed[0, :, columns].astype(jnp.float32)
        piece += outgoing[0, part].astype(jnp.float32)
        for source in range(1, n):
            piece += incoming[source, part].astype(jnp.float32)
        squares += jnp.sum(piece * piece, axis=-1, keepdims=True)
        parts.append(piece)
    factor = lax.rsqrt(squares / width + 1e-06)
    for part, piece in enumerate(parts):
        columns = slice(part * chunk, (part + 1) * chunk)
        out_ref[:, columns] = inputs[:, columns] + piece * factor * out_gain[:, columns]

    def sent(offset, _):
        gather_copy(offset).wait_send()
        reduce_copy(offset, None).wait_send()

    lax.fori_loop(1, n, sent, None)


def on_device(
    inputs,
    norm_gain,
    dense_gate,
    dense_up,
    dense_down,
    expert_gate,
    expert_up,
    expert_down,
    expert_ids,
    route_weights,
    out_gain,
):
    n = lax.axis_size("ep")
    own, width = inputs.shape
    rows = n * own
    cols_dense = dense_gate.shape[1]
    cols_expert = expert_gate.shape[1]
    n_dense = 0 if cols_dense % WIDE else cols_dense // WIDE
    n_expert = cols_expert // WIDE
    n_down = width // (WIDE * QUARTERS)
    spare_shape = (2, width, cols_dense) if n_dense == 0 else (2, 16, 128)
    fixed = 2 * spare_shape[0] * spare_shape[1] * -(-spare_shape[2] // 128) * 128
    fixed += rows * width * 2 * 4 + rows * WIDE * 4 * 8 + 2 * rows * (cols_dense + cols_expert) + (1 << 20)
    slots = min((VMEM_TOTAL - fixed) // (2 * width * WIDE * 2), n_dense + n_expert + n_down)
    cfg = (n, own, slots, n_dense, n_expert, n_down)
    n_parts = width // (2 * WIDE)
    anywhere = pl.BlockSpec(memory_space=pl.ANY)
    return pl.pallas_call(
        functools.partial(kernel, cfg),
        out_shape=jax.ShapeDtypeStruct((own, width), jnp.float32),
        in_specs=[anywhere] * 11,
        out_specs=pl.BlockSpec(memory_space=pltpu.VMEM),
        scratch_shapes=[
            pltpu.VMEM((own, width), jnp.float32),
            pltpu.VMEM((1, width), jnp.float32),
            pltpu.VMEM((1, width), jnp.float32),
            pltpu.VMEM(expert_ids.shape, jnp.int32),
            pltpu.VMEM(route_weights.shape, jnp.int32),
            pltpu.VMEM((slots, 2, width, WIDE), jnp.bfloat16),
            pltpu.VMEM(spare_shape, jnp.bfloat16),
            pltpu.VMEM((n, own, width), jnp.bfloat16),
            pltpu.VMEM((rows, width), jnp.bfloat16),
            pltpu.VMEM((rows, cols_dense), jnp.bfloat16),
            pltpu.VMEM((rows, cols_expert), jnp.bfloat16),
            pltpu.VMEM((2, n, own, WIDE), jnp.float32),
            pltpu.VMEM((rows, WIDE), jnp.float32),
            pltpu.VMEM((n, n_parts, own, 2 * WIDE), jnp.bfloat16),
            pltpu.VMEM((n, n_parts, own, 2 * WIDE), jnp.bfloat16),
            pltpu.SemaphoreType.DMA((5,)),
            pltpu.SemaphoreType.DMA((slots, 2 * QUARTERS)),
            pltpu.SemaphoreType.DMA((2,)),
            pltpu.SemaphoreType.DMA((n,)),
            pltpu.SemaphoreType.DMA((n,)),
            pltpu.SemaphoreType.DMA((n,)),
            pltpu.SemaphoreType.DMA((n,)),
        ],
        compiler_params=pltpu.CompilerParams(
            collective_id=0, has_side_effects=True, vmem_limit_bytes=67_043_328
        ),
        name="layer",
    )(
        inputs,
        norm_gain.reshape(1, width),
        dense_gate,
        dense_up,
        dense_down,
        expert_gate,
        expert_up,
        expert_down,
        expert_ids,
        route_weights,
        out_gain.reshape(1, width),
    )


def solution(mesh):
    placed = (
        P(("groups", "ep"), None),
        P(),
        P(None, "ep"),
        P(None, "ep"),
        P("ep", None),
        P(None, "ep"),
        P(None, "ep"),
        P("ep", None),
        P("groups", None),
        P("groups", None),
        P(),
    )
    return jax.shard_map(
        on_device, mesh=mesh, in_specs=placed, out_specs=P(("groups", "ep"), None), check_vma=False
    )
```

time: 183 us -> 60.4 us (0.33)
  waiting for transfers between devices: 88.7 us -> 0 us
  Pallas kernels: 0 us -> 55.9 us
  matrix products: 45.8 us -> 0 us
  blocking collectives: 24.2 us -> 0 us
  between operations: 14.2 us -> 0.01 us
  other arithmetic: 6.89 us -> 0 us
    unnamed x2 -> x0, waiting for transfers between devices: 88.7 us -> none
    pallas_call x0 -> x1, Pallas kernels: none -> 55.9 us  [on_device(): pl.pallas_call(functools.partial(kernel, cfg), out_shape=jax.ShapeDtypeSt...]
    dot_general x4 -> x0, matrix products: 45.8 us -> none  [the longest x1 19.9 us: on_device(): jnp.dot(e_hidden, expert_down, preferred_element_type=jnp.float32)]
    all_gather x1 -> x0, blocking collectives: 24.2 us -> none  [on_device(): gathered = lax.all_gather(hidden_in, 'ep', axis=0, tiled=True)]
    reduce_sum x6 -> x0, other arithmetic: 3.2 us -> none  [the longest x2 2.12 us: rms_scale(): jnp.mean(values * values, axis=-1, keepdims=True) + 1e-06]
    unnamed x14 -> x3, local copies, waits for them, and re-layouts: 1.67 us -> 4.18 us
  transfers between devices with their start and end apart: 1 -> 0, of which waited for: 1 -> 0; matrix products, arithmetic and copies ran while one was open for 0% -> 0% of each run, Pallas kernels for 0% -> 0%
where the time goes in v1:
time: 60.4 us; the launch traced here: 60.1 us
  Pallas kernels  55.9 us (93%)
  local copies, waits for them, and re-layouts  4.18 us (7%)
    pallas_call x1, Pallas kernels, on_device(): pl.pallas_call(functools.partial(kernel, cfg), out_shape=jax.ShapeDtypeSt...  55.9 us
    unnamed x3, local copies, waits for them, and re-layouts  4.18 us

profile of v1, /device:TPU:0, one launch (start us, length us, event | category | flops | bytes accessed | tf_op | source)
XLA Modules:
  0.0 60.1 jit_solution(5012196184654197300)
XLA Ops:
  0.0 1.4 %copy.12.ids_hbm = s32[32,12]{1,0:T(8,128)} copy(s32[32,12]{0,1:T(8,128)} %param.19) | data formatting | bytes 3072 | tf_op args[8]
  1.4 1.4 %copy.13.route_hbm = s32[32,12]{1,0:T(8,128)} copy(s32[32,12]{0,1:T(8,128)} %param.20) | data formatting | bytes 3072 | tf_op args[9]
  2.8 55.9 %layer.1 = f32[2,6144]{1,0:T(2,128)} custom-call(f32[2,6144]{1,0:T(2,128)} %inputs_hbm.1, f32[1,6144]{1,0:T(1,128)} %bitcast.2, bf16[6144,768]{1,0:T(8,128)(2,1)} %dense_gate.1, bf16[6144,768]{1,0:T(8,128)(2,1)} %dense_up.1, bf16[768,6144]{1,0:T(8,128)(2,1)} %dense_down.1, bf16[6144,2048]{1,0:T(8,128)(2,1)} %expert_gate.1, bf16[6144,2048]{1,0:T(8,128)(2,1)} %expert_up.1, ...), custom_call_target="tpu_custom_call" | custom-call | tf_op jit(solution)/shard_map/layer/pallas_call | solution.py:301
  58.7 1.4 %copy.15 = f32[2,6144]{1,0:T(2,128)} copy(f32[2,6144]{1,0:T(2,128)} %layer.1) | data formatting | bytes 98304

commit v2 on v1

v2 whole, which is shorter than its diff:
```python
import functools

import jax
import jax.numpy as jnp
from jax import lax
from jax.experimental import pallas as pl
from jax.experimental.pallas import tpu as pltpu
from jax.sharding import PartitionSpec as P

EXPERTS = 16
WIDE = 256
HALVES = 2
LAG = 3
VMEM_TOTAL = 66_000_000


def kernel(
    cfg,
    inputs_hbm,
    norm_gain_hbm,
    dense_gate,
    dense_up,
    dense_down,
    expert_gate,
    expert_up,
    expert_down,
    ids_hbm,
    route_hbm,
    out_gain_hbm,
    out_ref,
    inputs,
    norm_gain,
    out_gain,
    ids,
    route,
    ring,
    spare,
    landed,
    rows_in,
    dense_hidden,
    expert_hidden,
    scale,
    out_near,
    in_near,
    out_far,
    in_far,
    small_sem,
    ring_sem,
    spare_sem,
    gather_send,
    gather_recv,
    near_send,
    near_recv,
    far_send,
    far_recv,
):
    n, near, own, slots, n_dense, n_expert, n_down = cfg
    far = n // near
    rows = n * own
    width = inputs.shape[1]
    k_dense = dense_down.shape[0]
    k_expert = expert_down.shape[0]
    k_both = k_dense + k_expert
    n_up = n_dense + n_expert
    total = n_up + n_down
    me = lax.axis_index("ep")
    expert = me // (n // EXPERTS)
    my_far, my_near = me // near, lax.rem(me, near)

    def to_far(step):
        return {"ep": lax.rem(my_far + step, far) * near + my_near}

    def to_near(step):
        return {"ep": my_far * near + lax.rem(my_near + step, near)}

    def up_copies(unit, first, gate, upper):
        slot = lax.rem(unit, slots)
        columns = pl.ds(pl.multiple_of((unit - first) * WIDE, WIDE), WIDE)
        return [
            pltpu.make_async_copy(
                source.at[:, columns],
                ring.at[slot, :, pl.ds(which * WIDE, WIDE)],
                ring_sem.at[slot, which],
            )
            for which, source in enumerate((gate, upper))
        ]

    def down_copies(unit, half):
        slot = lax.rem(unit, slots)
        start = ((unit - n_up) * HALVES + half) * (2 * WIDE)
        columns = pl.ds(pl.multiple_of(start, 2 * WIDE), 2 * WIDE)
        base = half * k_both
        return [
            pltpu.make_async_copy(
                dense_down.at[:, columns],
                ring.at[slot, pl.ds(base, k_dense)],
                ring_sem.at[slot, 2 * half],
            ),
            pltpu.make_async_copy(
                expert_down.at[:, columns],
                ring.at[slot, pl.ds(base + k_dense, k_expert)],
                ring_sem.at[slot, 2 * half + 1],
            ),
        ]

    def start_unit(unit):
        @pl.when(unit < n_dense)
        def _():
            for copy in up_copies(unit, 0, dense_gate, dense_up):
                copy.start()

        @pl.when((unit >= n_dense) & (unit < n_up))
        def _():
            for copy in up_copies(unit, n_dense, expert_gate, expert_up):
                copy.start()

        @pl.when((unit >= n_up) & (unit < total))
        def _():
            for half in range(HALVES):
                for copy in down_copies(unit, half):
                    copy.start()

    small = [
        pltpu.make_async_copy(source, target, small_sem.at[at])
        for at, (source, target) in enumerate(
            (
                (inputs_hbm, inputs),
                (norm_gain_hbm, norm_gain),
                (ids_hbm, ids),
                (route_hbm, route),
                (out_gain_hbm, out_gain),
            )
        )
    ]
    for copy in small:
        copy.start()
    if n_dense == 0:
        spare_copies = [
            pltpu.make_async_copy(source, spare.at[at], spare_sem.at[at])
            for at, source in enumerate((dense_gate, dense_up))
        ]
        for copy in spare_copies:
            copy.start()
    lax.fori_loop(0, min(slots, total), lambda unit, _: start_unit(unit), None)

    barrier = pltpu.get_barrier_semaphore()

    for step in range(1, far):
        pl.semaphore_signal(barrier, inc=1, device_id=to_far(step))
    for step in range(1, near):
        pl.semaphore_signal(barrier, inc=1, device_id=to_near(step))

    for copy in small:
        copy.wait()
    value = inputs[...]
    square = jnp.mean(value * value, axis=-1, keepdims=True)
    hidden_own = (value * lax.rsqrt(square + 1e-06) * norm_gain[...]).astype(jnp.bfloat16)
    landed[0] = hidden_own
    pl.semaphore_wait(barrier, far + near - 2)

    def gather_far(step):
        return pltpu.make_async_remote_copy(
            src_ref=landed.at[0],
            dst_ref=landed.at[(far - step) * near],
            send_sem=gather_send.at[step * near],
            recv_sem=gather_recv.at[(far - step) * near],
            device_id=to_far(step),
        )

    def gather_near(step, hop):
        return pltpu.make_async_remote_copy(
            src_ref=landed.at[step * near],
            dst_ref=landed.at[step * near + near - hop],
            send_sem=gather_send.at[step * near + hop],
            recv_sem=gather_recv.at[step * near + near - hop],
            device_id=to_near(hop),
        )

    for step in range(1, far):
        gather_far(step).start()
    for hop in range(1, near):
        gather_near(0, hop).start()

    weights_all = route[...].astype(jnp.float32) / 1024.0
    named = jnp.sum(jnp.where(ids[...] == expert, weights_all, 0.0), axis=0, keepdims=True)
    zeros = jnp.sum(jnp.where(ids[...] == EXPERTS, weights_all, 0.0), axis=0, keepdims=True)
    line = lax.broadcasted_iota(jnp.int32, (rows, rows), 0)
    block, inside = line // own, lax.rem(line, own)
    source_far = lax.rem(my_far + block // near, far)
    source_near = lax.rem(my_near + lax.rem(block, near), near)
    source = (source_far * near + source_near) * own + inside
    column = lax.broadcasted_iota(jnp.int32, (rows, rows), 1)
    weight = jnp.sum(jnp.where(column == source, named, 0.0), axis=1, keepdims=True)
    scale[...] = jnp.broadcast_to(weight, scale.shape)
    own_line = lax.broadcasted_iota(jnp.int32, (own, rows), 0) + me * own
    own_column = lax.broadcasted_iota(jnp.int32, (own, rows), 1)
    zero_weight = jnp.sum(jnp.where(own_column == own_line, zeros, 0.0), axis=1, keepdims=True)

    def place(block):
        rows_in[block * own : (block + 1) * own] = landed[block]

    place(0)
    for step in range(1, far):
        gather_far(far - step).wait_recv()
        for hop in range(1, near):
            gather_near(step, hop).start()
        place(step * near)
    for step in range(far):
        for hop in range(1, near):
            gather_near(step, near - hop).wait_recv()
            place(step * near + hop)

    def gated(gate, upper):
        return (gate / (1.0 + jnp.exp(-gate)) * upper).astype(jnp.bfloat16)

    def product(left, right):
        return jnp.dot(left, right, preferred_element_type=jnp.float32)

    def up_unit(first, gate_hbm, upper_hbm, hidden):
        def body(unit, _):
            slot = lax.rem(unit, slots)
            copies = up_copies(unit, first, gate_hbm, upper_hbm)
            for copy in copies:
                copy.wait()
            both = product(rows_in[...], ring[slot])
            gate, upper = both[:, :WIDE], both[:, WIDE:]
            columns = pl.ds(pl.multiple_of((unit - first) * WIDE, WIDE), WIDE)
            hidden[:, columns] = gated(gate, upper)
            start_unit(unit + slots)

        return body

    if n_dense == 0:
        for copy in spare_copies:
            copy.wait()
        dense_hidden[...] = gated(
            product(rows_in[...], spare[0]), product(rows_in[...], spare[1])
        )
    else:
        lax.fori_loop(0, n_dense, up_unit(0, dense_gate, dense_up, dense_hidden), None)
    lax.fori_loop(n_dense, n_up, up_unit(n_dense, expert_gate, expert_up, expert_hidden), None)

    n_parts = width // (2 * WIDE)

    def near_copy(hop, part):
        source, target = out_near.at[hop], in_near.at[near - hop]
        if part is not None:
            source, target = out_near.at[hop, part], in_near.at[near - hop, part]
        return pltpu.make_async_remote_copy(
            src_ref=source,
            dst_ref=target,
            send_sem=near_send.at[hop],
            recv_sem=near_recv.at[near - hop, 0 if part is None else part],
            device_id=to_near(hop),
        )

    def far_copy(step, part):
        source, target = out_far.at[step], in_far.at[far - step]
        if part is not None:
            source, target = out_far.at[step, part], in_far.at[far - step, part]
        return pltpu.make_async_remote_copy(
            src_ref=source,
            dst_ref=target,
            send_sem=far_send.at[step],
            recv_sem=far_recv.at[far - step],
            device_id=to_far(step),
        )

    def pass_on(part):
        for hop in range(1, near):
            near_copy(near - hop, part).wait_recv()
        for step in range(far):
            piece = out_near[0, part, step].astype(jnp.float32)
            for hop in range(1, near):
                piece += in_near[hop, part, step].astype(jnp.float32)
            out_far[step, part] = piece.astype(out_far.dtype)
        for step in range(1, far):
            far_copy(step, part).start()

    def down_unit(unit, _):
        slot = lax.rem(unit, slots)
        weight = scale[...]
        for half in range(HALVES):
            for copy in down_copies(unit, half):
                copy.wait()
            base = half * k_both
            block = ring.at[slot]
            part_sum = product(dense_hidden[...], block[base : base + k_dense])
            part_sum += weight * product(
                expert_hidden[...], block[base + k_dense : base + k_both]
            )
            part = (unit - n_up) * HALVES + half
            for to in range(n):
                out_near[to % near, part, to // near] = part_sum[
                    to * own : (to + 1) * own
                ].astype(jnp.bfloat16)
            for hop in range(1, near):
                near_copy(hop, part).start()

            @pl.when(part >= LAG)
            def _():
                pass_on(part - LAG)

        start_unit(unit + slots)

    lax.fori_loop(n_up, total, down_unit, None)

    lax.fori_loop(n_parts - LAG, n_parts, lambda part, _: pass_on(part), None)
    for step in range(1, far):
        far_copy(far - step, None).wait_recv()
    parts = []
    chunk = 2 * WIDE
    squares = jnp.zeros((own, 1), jnp.float32)
    for part in range(width // chunk):
        columns = slice(part * chunk, (part + 1) * chunk)
        piece = zero_weight * landed[0, :, columns].astype(jnp.float32)
        piece += out_far[0, part].astype(jnp.float32)
        for step in range(1, far):
            piece += in_far[step, part].astype(jnp.float32)
        squares += jnp.sum(piece * piece, axis=-1, keepdims=True)
        parts.append(piece)
    factor = lax.rsqrt(squares / width + 1e-06)
    for part, piece in enumerate(parts):
        columns = slice(part * chunk, (part + 1) * chunk)
        out_ref[:, columns] = inputs[:, columns] + piece * factor * out_gain[:, columns]

    for step in range(1, far):
        gather_far(step).wait_send()
        far_copy(step, None).wait_send()
    for hop in range(1, near):
        for step in range(far):
            gather_near(step, hop).wait_send()
        near_copy(hop, None).wait_send()


def on_device(
    inputs,
    norm_gain,
    dense_gate,
    dense_up,
    dense_down,
    expert_gate,
    expert_up,
    expert_down,
    expert_ids,
    route_weights,
    out_gain,
):
    n = lax.axis_size("ep")
    own, width = inputs.shape
    rows = n * own
    cols_dense = dense_gate.shape[1]
    cols_expert = expert_gate.shape[1]
    n_dense = 0 if cols_dense % WIDE else cols_dense // WIDE
    n_expert = cols_expert // WIDE
    n_down = width // (2 * WIDE * HALVES)
    spare_shape = (2, width, cols_dense) if n_dense == 0 else (2, 16, 128)
    fixed = 2 * spare_shape[0] * spare_shape[1] * -(-spare_shape[2] // 128) * 128
    fixed += rows * width * 2 * 4 + rows * WIDE * 4 * 8 + 2 * rows * (cols_dense + cols_expert) + (1 << 20)
    slots = min((VMEM_TOTAL - fixed) // (2 * width * WIDE * 2), n_dense + n_expert + n_down)
    near = 1
    while near * near < n:
        near *= 2
    far = n // near
    cfg = (n, near, own, slots, n_dense, n_expert, n_down)
    n_parts = width // (2 * WIDE)
    anywhere = pl.BlockSpec(memory_space=pl.ANY)
    return pl.pallas_call(
        functools.partial(kernel, cfg),
        out_shape=jax.ShapeDtypeStruct((own, width), jnp.float32),
        in_specs=[anywhere] * 11,
        out_specs=pl.BlockSpec(memory_space=pltpu.VMEM),
        scratch_shapes=[
            pltpu.VMEM((own, width), jnp.float32),
            pltpu.VMEM((1, width), jnp.float32),
            pltpu.VMEM((1, width), jnp.float32),
            pltpu.VMEM(expert_ids.shape[::-1], jnp.int32),
            pltpu.VMEM(route_weights.shape[::-1], jnp.int32),
            pltpu.VMEM((slots, width, 2 * WIDE), jnp.bfloat16),
            pltpu.VMEM(spare_shape, jnp.bfloat16),
            pltpu.VMEM((n, own, width), jnp.bfloat16),
            pltpu.VMEM((rows, width), jnp.bfloat16),
            pltpu.VMEM((rows, cols_dense), jnp.bfloat16),
            pltpu.VMEM((rows, cols_expert), jnp.bfloat16),
            pltpu.VMEM((rows, 2 * WIDE), jnp.float32),
            pltpu.VMEM((near, n_parts, far, own, 2 * WIDE), jnp.bfloat16),
            pltpu.VMEM((near, n_parts, far, own, 2 * WIDE), jnp.bfloat16),
            pltpu.VMEM((far, n_parts, own, 2 * WIDE), jnp.bfloat16),
            pltpu.VMEM((far, n_parts, own, 2 * WIDE), jnp.bfloat16),
            pltpu.SemaphoreType.DMA((5,)),
            pltpu.SemaphoreType.DMA((slots, 2 * HALVES)),
            pltpu.SemaphoreType.DMA((2,)),
            pltpu.SemaphoreType.DMA((n,)),
            pltpu.SemaphoreType.DMA((n,)),
            pltpu.SemaphoreType.DMA((near,)),
            pltpu.SemaphoreType.DMA((near, n_parts)),
            pltpu.SemaphoreType.DMA((far,)),
            pltpu.SemaphoreType.DMA((far,)),
        ],
        compiler_params=pltpu.CompilerParams(
            collective_id=0, has_side_effects=True, vmem_limit_bytes=67_043_328
        ),
        name="layer",
    )(
        inputs,
        norm_gain.reshape(1, width),
        dense_gate,
        dense_up,
        dense_down,
        expert_gate,
        expert_up,
        expert_down,
        expert_ids.T,
        route_weights.T,
        out_gain.reshape(1, width),
    )


def solution(mesh):
    placed = (
        P(("groups", "ep"), None),
        P(),
        P(None, "ep"),
        P(None, "ep"),
        P("ep", None),
        P(None, "ep"),
        P(None, "ep"),
        P("ep", None),
        P("groups", None),
        P("groups", None),
        P(),
    )
    return jax.shard_map(
        on_device, mesh=mesh, in_specs=placed, out_specs=P(("groups", "ep"), None), check_vma=False
    )
```

time: 60.4 us -> 45.8 us (0.76)
  Pallas kernels: 55.9 us -> 44.2 us
  local copies, waits for them, and re-layouts: 4.18 us -> 1.42 us
    pallas_call x1, Pallas kernels: 55.9 us -> 44.2 us  [on_device(): pl.pallas_call(functools.partial(kernel, cfg), out_shape=jax.ShapeDtypeSt...]
    unnamed x3 -> x1, local copies, waits for them, and re-layouts: 4.18 us -> 1.42 us
where the time goes in v2:
time: 45.8 us; the launch traced here: 45.6 us
  Pallas kernels  44.2 us (97%)
  local copies, waits for them, and re-layouts  1.42 us (3%)
    pallas_call x1, Pallas kernels, on_device(): pl.pallas_call(functools.partial(kernel, cfg), out_shape=jax.ShapeDtypeSt...  44.2 us
    unnamed x1, local copies, waits for them, and re-layouts  1.42 us

profile of v2, /device:TPU:0, one launch (start us, length us, event | category | flops | bytes accessed | tf_op | source)
XLA Modules:
  0.0 45.6 jit_solution(12212636859836373949)
XLA Ops:
  0.0 44.2 %layer.1 = f32[2,6144]{1,0:T(2,128)} custom-call(f32[2,6144]{1,0:T(2,128)} %inputs_hbm.1, f32[1,6144]{1,0:T(1,128)} %bitcast.4, bf16[6144,768]{1,0:T(8,128)(2,1)} %dense_gate.1, bf16[6144,768]{1,0:T(8,128)(2,1)} %dense_up.1, bf16[768,6144]{1,0:T(8,128)(2,1)} %dense_down.1, bf16[6144,2048]{1,0:T(8,128)(2,1)} %expert_gate.1, bf16[6144,2048]{1,0:T(8,128)(2,1)} %expert_up.1, ...), custom_call_target="tpu_custom_call" | custom-call | tf_op jit(solution)/shard_map/layer/pallas_call | solution.py:368
  44.2 1.4 %copy.13 = f32[2,6144]{1,0:T(2,128)} copy(f32[2,6144]{1,0:T(2,128)} %layer.1) | data formatting | bytes 98304

commit v3 on v2

--- a/solution.py
+++ b/solution.py
@@ -10,6 +10,7 @@
 EXPERTS = 16
 WIDE = 256
 HALVES = 2
+DIRECT = 2
 LAG = 3
 VMEM_TOTAL = 66_000_000
 
@@ -44,6 +45,8 @@
     in_near,
     out_far,
     in_far,
+    out_direct,
+    in_direct,
     small_sem,
     ring_sem,
     spare_sem,
@@ -53,6 +56,8 @@
     near_recv,
     far_send,
     far_recv,
+    direct_send,
+    direct_recv,
 ):
     n, near, own, slots, n_dense, n_expert, n_down = cfg
     far = n // near
@@ -145,10 +150,10 @@
 
     barrier = pltpu.get_barrier_semaphore()
 
-    for step in range(1, far):
-        pl.semaphore_signal(barrier, inc=1, device_id=to_far(step))
-    for step in range(1, near):
-        pl.semaphore_signal(barrier, inc=1, device_id=to_near(step))
+    def greet(offset, _):
+        pl.semaphore_signal(barrier, inc=1, device_id={"ep": lax.rem(me + offset, n)})
+
+    lax.fori_loop(1, n, greet, None)
 
     for copy in small:
         copy.wait()
@@ -156,7 +161,7 @@
     square = jnp.mean(value * value, axis=-1, keepdims=True)
     hidden_own = (value * lax.rsqrt(square + 1e-06) * norm_gain[...]).astype(jnp.bfloat16)
     landed[0] = hidden_own
-    pl.semaphore_wait(barrier, far + near - 2)
+    pl.semaphore_wait(barrier, n - 1)
 
     def gather_far(step):
         return pltpu.make_async_remote_copy(
@@ -241,6 +246,22 @@
     lax.fori_loop(n_dense, n_up, up_unit(n_dense, expert_gate, expert_up, expert_hidden), None)
 
     n_parts = width // (2 * WIDE)
+    n_hops = n_parts - DIRECT * HALVES
+
+    def direct_copy(block, part):
+        there_far, there_near = block // near, lax.rem(block, near)
+        back = lax.rem(far - there_far, far) * near + lax.rem(near - there_near, near)
+        source, target = out_direct.at[block], in_direct.at[back]
+        if part is not None:
+            source, target = out_direct.at[block, part], in_direct.at[back, part]
+        to = lax.rem(my_far + there_far, far) * near + lax.rem(my_near + there_near, near)
+        return pltpu.make_async_remote_copy(
+            src_ref=source,
+            dst_ref=target,
+            send_sem=direct_send.at[block],
+            recv_sem=direct_recv.at[back],
+            device_id={"ep": to},
+        )
 
     def near_copy(hop, part):
         source, target = out_near.at[hop], in_near.at[near - hop]
@@ -303,20 +324,59 @@
 
         start_unit(unit + slots)
 
-    lax.fori_loop(n_up, total, down_unit, None)
-
-    lax.fori_loop(n_parts - LAG, n_parts, lambda part, _: pass_on(part), None)
+    def direct_unit(unit, _):
+        slot = lax.rem(unit, slots)
+        weight = scale[...]
+        for half in range(HALVES):
+            for copy in down_copies(unit, half):
+                copy.wait()
+            base = half * k_both
+            block = ring.at[slot]
+            part_sum = product(dense_hidden[...], block[base : base + k_dense])
+            part_sum += weight * product(
+                expert_hidden[...], block[base + k_dense : base + k_both]
+            )
+            part = (unit - n_up) * HALVES + half
+            for to in range(n):
+                out_direct[to, part - n_hops] = part_sum[to * own : (to + 1) * own].astype(
+                    jnp.bfloat16
+                )
+            lax.fori_loop(
+                1, n, lambda block, _: direct_copy(block, part - n_hops).start(), None
+            )
+
+            @pl.when(part - LAG < n_hops)
+            def _():
+                pass_on(part - LAG)
+
+        start_unit(unit + slots)
+
+    lax.fori_loop(n_up, total - DIRECT, down_unit, None)
+    lax.fori_loop(total - DIRECT, total, direct_unit, None)
+
     for step in range(1, far):
         far_copy(far - step, None).wait_recv()
+
+    def landed_direct(block, _):
+        direct_copy(block, None).wait_recv()
+
+    def sent_direct(block, _):
+        direct_copy(block, None).wait_send()
+
     parts = []
     chunk = 2 * WIDE
     squares = jnp.zeros((own, 1), jnp.float32)
     for part in range(width // chunk):
         columns = slice(part * chunk, (part + 1) * chunk)
         piece = zero_weight * landed[0, :, columns].astype(jnp.float32)
-        piece += out_far[0, part].astype(jnp.float32)
-        for step in range(1, far):
-            piece += in_far[step, part].astype(jnp.float32)
+        if part == n_hops:
+            lax.fori_loop(1, n, landed_direct, None)
+        own_part, others, at = out_far, in_far, part
+        if part >= n_hops:
+            own_part, others, at = out_direct, in_direct, part - n_hops
+        piece += own_part[0, at].astype(jnp.float32)
+        for step in range(1, others.shape[0]):
+            piece += others[step, at].astype(jnp.float32)
         squares += jnp.sum(piece * piece, axis=-1, keepdims=True)
         parts.append(piece)
     factor = lax.rsqrt(squares / width + 1e-06)
@@ -331,6 +391,7 @@
         for step in range(far):
             gather_near(step, hop).wait_send()
         near_copy(hop, None).wait_send()
+    lax.fori_loop(1, n, sent_direct, None)
 
 
 def on_device(
@@ -364,6 +425,7 @@
     far = n // near
     cfg = (n, near, own, slots, n_dense, n_expert, n_down)
     n_parts = width // (2 * WIDE)
+    n_hops = n_parts - DIRECT * HALVES
     anywhere = pl.BlockSpec(memory_space=pl.ANY)
     return pl.pallas_call(
         functools.partial(kernel, cfg),
@@ -383,19 +445,23 @@
             pltpu.VMEM((rows, cols_dense), jnp.bfloat16),
             pltpu.VMEM((rows, cols_expert), jnp.bfloat16),
             pltpu.VMEM((rows, 2 * WIDE), jnp.float32),
-            pltpu.VMEM((near, n_parts, far, own, 2 * WIDE), jnp.bfloat16),
-            pltpu.VMEM((near, n_parts, far, own, 2 * WIDE), jnp.bfloat16),
-            pltpu.VMEM((far, n_parts, own, 2 * WIDE), jnp.bfloat16),
-            pltpu.VMEM((far, n_parts, own, 2 * WIDE), jnp.bfloat16),
+            pltpu.VMEM((near, n_hops, far, own, 2 * WIDE), jnp.bfloat16),
+            pltpu.VMEM((near, n_hops, far, own, 2 * WIDE), jnp.bfloat16),
+            pltpu.VMEM((far, n_hops, own, 2 * WIDE), jnp.bfloat16),
+            pltpu.VMEM((far, n_hops, own, 2 * WIDE), jnp.bfloat16),
+            pltpu.VMEM((n, n_parts - n_hops, own, 2 * WIDE), jnp.bfloat16),
+            pltpu.VMEM((n, n_parts - n_hops, own, 2 * WIDE), jnp.bfloat16),
             pltpu.SemaphoreType.DMA((5,)),
             pltpu.SemaphoreType.DMA((slots, 2 * HALVES)),
             pltpu.SemaphoreType.DMA((2,)),
             pltpu.SemaphoreType.DMA((n,)),
             pltpu.SemaphoreType.DMA((n,)),
             pltpu.SemaphoreType.DMA((near,)),
-            pltpu.SemaphoreType.DMA((near, n_parts)),
+            pltpu.SemaphoreType.DMA((near, n_hops)),
             pltpu.SemaphoreType.DMA((far,)),
             pltpu.SemaphoreType.DMA((far,)),
+            pltpu.SemaphoreType.DMA((n,)),
+            pltpu.SemaphoreType.DMA((n,)),
         ],
         compiler_params=pltpu.CompilerParams(
             collective_id=0, has_side_effects=True, vmem_limit_bytes=67_043_328

time: 45.8 us -> 46.3 us (1.011)
  Pallas kernels: 44.2 us -> 44.7 us
    pallas_call x1, Pallas kernels: 44.2 us -> 44.7 us  [on_device(): pl.pallas_call(functools.partial(kernel, cfg), out_shape=jax.ShapeDtypeSt...]
where the time goes in v3:
time: 46.3 us; the launch traced here: 46.2 us
  Pallas kernels  44.7 us (97%)
  local copies, waits for them, and re-layouts  1.42 us (3%)
    pallas_call x1, Pallas kernels, on_device(): pl.pallas_call(functools.partial(kernel, cfg), out_shape=jax.ShapeDtypeSt...  44.7 us
    unnamed x1, local copies, waits for them, and re-layouts  1.42 us

profile of v3, /device:TPU:0, one launch (start us, length us, event | category | flops | bytes accessed | tf_op | source)
XLA Modules:
  0.0 46.2 jit_solution(14129299967477745238)
XLA Ops:
  0.0 44.7 %layer.1 = f32[2,6144]{1,0:T(2,128)} custom-call(f32[2,6144]{1,0:T(2,128)} %inputs_hbm.1, f32[1,6144]{1,0:T(1,128)} %bitcast.4, bf16[6144,768]{1,0:T(8,128)(2,1)} %dense_gate.1, bf16[6144,768]{1,0:T(8,128)(2,1)} %dense_up.1, bf16[768,6144]{1,0:T(8,128)(2,1)} %dense_down.1, bf16[6144,2048]{1,0:T(8,128)(2,1)} %expert_gate.1, bf16[6144,2048]{1,0:T(8,128)(2,1)} %expert_up.1, ...), custom_call_target="tpu_custom_call" | custom-call | tf_op jit(solution)/shard_map/layer/pallas_call | solution.py:430
  44.7 1.4 %copy.13 = f32[2,6144]{1,0:T(2,128)} copy(f32[2,6144]{1,0:T(2,128)} %layer.1) | data formatting | bytes 98304
